TPU v7x, 32 devices: a whole 2x2x4 slice. The times are simulated.
32 devices in a mesh: groups: 2 (over y), space: 4 (over z), tm: 2 (over x), col: 2 (over core).
Axes of the slice: x: 2, y: 2, z: 4, core: 2. Of those that a mesh axis runs over, the one named last changes fastest.
Arguments:
- activations: bfloat16 [4, 16, 512, 256], P(('groups', 'tm'), ('space', 'col')), parts along dimension 0, may hold values from -6 to 6
- conv_weight: bfloat16 [3, 3, 256, 256], replicated, may hold values from -0.125 to 0.125
- conv_bias: float32 [256], replicated, may hold values from -3 to 3
- head_weight: bfloat16 [256, 32], replicated, may hold values from -0.375 to 0.375
- latent_grad: bfloat16 [4, 8, 256, 16], P(('groups', 'tm'), None, ('space', 'col')), parts along dimension 0, may hold values from -6 to 6
- noise_sample: bfloat16 [4, 8, 256, 16], P(('groups', 'tm'), ('space', 'col')), parts along dimension 0, may hold values from -5 to 5
Outputs:
- x_grad: bfloat16 [4, 16, 512, 256], P(('groups', 'tm'), ('space', 'col')), parts along dimension 0
- conv_weight_grad: float32 [3, 3, 512, 256], P(None, None, ('groups', 'space', 'col')), parts along dimension 2
- head_weight_grad: float32 [512, 32], P(('groups', 'space', 'col')), parts along dimension 0
- conv_bias_grad: float32 [512], P(('groups', 'space', 'col')), parts along dimension 0
There are 2 independent parts, one for each index of `groups`. A program takes and returns all parts, laid end to end along the dimension named above; an argument that names none is the same for every part. Nothing has to cross between parts.
All inputs are finite; a program needn't handle non-finite values.
Results may differ from a plain program's by a relative error of at most 0.007.
Values may be sent and summed in bfloat16 or wider, within the bound.
No kernel may reach another device: no remote copies, remote signals or barrier semaphores. Data moves between devices by JAX's collectives and lax.ppermute only.
A program may use at most 64 MiB of HBM per device.

v0:
```python
import math
import jax
import jax.numpy as jnp
from jax import lax
from jax.sharding import PartitionSpec as P

kl_weight = 1.0


def passed_along(x, axis, by):
    peers = lax.axis_size(axis)
    pairs = [(i, i + by) for i in range(peers) if 0 <= i + by < peers]
    return lax.ppermute(x, axis, pairs)


def window_at(padded, index, row_count, col_count):
    row_tap = index // 3
    col_tap = index % 3
    return padded[:, row_tap : row_tap + 2 * row_count : 2, col_tap : col_tap + 2 * col_count : 2]


def parity_gradient(pre_grad, conv_weight, row_count, col_count):
    frames = pre_grad.shape[0]
    channels = conv_weight.shape[2]
    planes = {}
    for index in range(9):
        row_tap = index // 3
        col_tap = index % 3
        contrib = jnp.einsum(
            "trco,ko->trck",
            pre_grad,
            conv_weight[row_tap, col_tap],
            preferred_element_type=jnp.float32,
        )
        placed = jnp.pad(
            contrib,
            ((0, 0), (row_tap // 2, 1 - row_tap // 2), (col_tap // 2, 1 - col_tap // 2), (0, 0)),
        )
        parity = (row_tap % 2, col_tap % 2)
        if parity in planes:
            planes[parity] = planes[parity] + placed
        else:
            planes[parity] = placed
    even_rows = jnp.stack([planes[0, 0], planes[0, 1]], 3).reshape(
        frames, row_count + 1, 2 * col_count + 2, channels
    )
    odd_rows = jnp.stack([planes[1, 0], planes[1, 1]], 3).reshape(
        frames, row_count + 1, 2 * col_count + 2, channels
    )
    woven = jnp.stack([even_rows, odd_rows], 2).reshape(
        frames, 2 * row_count + 2, 2 * col_count + 2, channels
    )
    return woven[:, : 2 * row_count + 1, : 2 * col_count + 1]


def body(activations, conv_weight, conv_bias, head_weight, latent_grad, noise_sample):
    frames, double_rows, double_cols, channels = activations.shape
    row_count = double_rows // 2
    col_count = double_cols // 2
    latent_dim = latent_grad.shape[-1]
    upstream = lax.all_to_all(
        latent_grad, ("space", "col"), split_axis=1, concat_axis=2, tiled=True
    )
    next_row = passed_along(activations[:, :1], ("space", "col"), -1)
    padded = jnp.pad(jnp.concatenate([activations, next_row], 1), ((0, 0), (0, 0), (0, 1), (0, 0)))
    pre_act = jnp.zeros((frames, row_count, col_count, channels), jnp.float32) + conv_bias
    for index in range(9):
        pre_act = pre_act + jnp.einsum(
            "trck,ko->trco",
            window_at(padded, index, row_count, col_count),
            conv_weight[index // 3, index % 3],
            preferred_element_type=jnp.float32,
        )
    hidden = jax.nn.silu(pre_act).astype(jnp.bfloat16)
    flattened = hidden.reshape(-1, channels)
    moments = jnp.dot(flattened, head_weight, preferred_element_type=jnp.float32)
    mean_part = moments[:, :latent_dim]
    logvar = moments[:, latent_dim:]
    upstream_flat = upstream.reshape(-1, latent_dim).astype(jnp.float32)
    sample = noise_sample.reshape(-1, latent_dim).astype(jnp.float32)
    spread = jnp.exp(0.5 * logvar)
    mean_grad = upstream_flat + kl_weight * mean_part
    logvar_grad = 0.5 * upstream_flat * sample * spread + 0.5 * kl_weight * (spread * spread - 1.0)
    moment_grad = jnp.concatenate([mean_grad, logvar_grad], 1).astype(jnp.bfloat16)
    head_term = jnp.dot(flattened.T, moment_grad, preferred_element_type=jnp.float32)
    hidden_grad = jnp.dot(moment_grad, head_weight.T, preferred_element_type=jnp.float32)
    hidden_grad = hidden_grad.reshape(frames, row_count, col_count, channels)
    gating = jax.nn.sigmoid(pre_act)
    pre_grad = (hidden_grad * gating * (1.0 + pre_act * (1.0 - gating))).astype(jnp.bfloat16)
    bias_term = jnp.sum(pre_grad, axis=(0, 1, 2), dtype=jnp.float32)
    kernel_terms = []
    for index in range(9):
        kernel_terms.append(
            jnp.einsum(
                "trck,trco->ko",
                window_at(padded, index, row_count, col_count),
                pre_grad,
                preferred_element_type=jnp.float32,
            )
        )
    kernel_term = jnp.stack(kernel_terms, 1).reshape(channels, 3, 3, channels)
    input_grad = parity_gradient(pre_grad, conv_weight, row_count, col_count)
    own_grad = input_grad[:, : 2 * row_count, : 2 * col_count]
    rim_grad = passed_along(input_grad[:, 2 * row_count :, : 2 * col_count], ("space", "col"), 1)
    own_grad = own_grad.at[:, :1].add(rim_grad)
    x_grad = own_grad.astype(jnp.bfloat16)
    totals = (
        lax.psum(kernel_term.astype(jnp.bfloat16), "tm").astype(jnp.float32),
        lax.psum(head_term.astype(jnp.bfloat16), "tm").astype(jnp.float32),
        lax.psum(bias_term.astype(jnp.bfloat16), "tm").astype(jnp.float32),
    )
    shares = (
        lax.psum_scatter(totals[0], ("space", "col"), scatter_dimension=0, tiled=True),
        lax.psum_scatter(totals[1], ("space", "col"), scatter_dimension=0, tiled=True),
        lax.psum_scatter(totals[2], ("space", "col"), scatter_dimension=0, tiled=True),
    )
    positions = (
        frames * lax.axis_size("tm") * row_count * lax.axis_size(("space", "col")) * col_count
    )
    grad_scale = 1.0 / math.sqrt(positions)
    kernel_grad = jnp.transpose(shares[0] * grad_scale, (1, 2, 0, 3))
    return (x_grad, kernel_grad, shares[1] * grad_scale, shares[2] * grad_scale)


def solution(mesh):
    in_specs = (
        P(("groups", "tm"), ("space", "col"), None, None),
        P(),
        P(),
        P(),
        P(("groups", "tm"), None, ("space", "col"), None),
        P(("groups", "tm"), ("space", "col"), None, None),
    )
    out_specs = (
        P(("groups", "tm"), ("space", "col"), None, None),
        P(None, None, ("groups", "space", "col"), None),
        P(("groups", "space", "col"), None),
        P(("groups", "space", "col")),
    )
    return jax.shard_map(body, mesh=mesh, in_specs=in_specs, out_specs=out_specs, check_vma=False)
```

profile of v0, /device:TPU:0, one launch (start us, length us, event | category | flops | bytes accessed | tf_op | source)
XLA Modules:
  0.0 126.6 jit_solution(13419863196311703334)
XLA Ops:
  8.1 1.0 slice.129
  9.1 1.3 %collective-permute-start = (bf16[1,1,512,256]{3,2,1,0:T(8,128)(2,1)S(1)}, bf16[1,1,512,256]{3,2,1,0:T(8,128)(2,1)S(1)}, u32[]{:S(2)}, u32[]{:S(2)}) collective-permute-start(bf16[1,1,512,256]{3,2,1,0:T(8,128)(2,1)S(1)} %slice.129), channel_id=1, source_target_pairs={{1,0},{4,1},{5,4},{8,5},{9,8},{12,9},{13,12},{3,2},{6,3},{7,6},{10... | collective-permute-start | bytes 786440 | tf_op jit(solution)/shard_map/ppermute | solution.py:13
  10.5 12.5 %all_to_all.4 = bf16[8,2,256]{2,1,0:T(2,128)(2,1)S(1)} all-to-all(bf16[8,2,256]{2,1,0:T(2,128)(2,1)S(1)} %reshape.190), channel_id=1, replica_groups=mesh['groups'=2,'space'=4,'tm'=2,'col'=2] {'space','col'}, dimensions={0} | all-to-all | bytes 16384 | tf_op jit(solution)/shard_map/all_to_all | solution.py:61
  23.3 0.4 slice.130
  23.7 0.4 slice.132
  24.1 0.4 slice.134
  24.5 0.4 slice.136
  24.9 0.4 slice.138
  25.3 0.4 slice.140
  25.8 0.4 slice.142
  26.2 0.4 slice.144
  26.6 0.4 slice.146
  28.7 0.2 multiply_convert_fusion
  29.4 0.2 fusion.85
  29.6 0.3 copy-done.9
  32.0 1.0 copy-done.3
  33.3 10.3 %all-reduce.11 = (bf16[256,32]{1,0:T(8,128)(2,1)S(1)}, bf16[256]{0:T(256)(128)(2,1)S(1)}) all-reduce(bf16[256,32]{1,0:T(8,128)(2,1)S(1)} %convolution_convert_fusion.9, bf16[256]{0:T(256)(128)(2,1)S(1)} %get-tuple-element.22), channel_id=1, replica_groups=mesh['groups'=2,'space'=4,'tm'=2,'col'=2] {'tm'}, use_global_device_ids=true, to_apply=%region_2.3 | all-reduce | flops 8448 | bytes 33792 | tf_op jit(solution)/shard_map/psum | solution.py:109
  43.6 0.7 convert_element_type.67
  44.4 30.4 %all-reduce.14.cloned.1.call-done = bf16[256,3,3,256]{3,0,2,1:T(8,128)(2,1)} async-done(((bf16[256,3,3,256]{3,0,2,1:T(8,128)(2,1)}), bf16[256,3,3,256]{3,0,2,1:T(8,128)(2,1)}) %all-reduce.14.cloned.1.call-update) | async-done | bytes 1179664 | tf_op jit(solution)/shard_map/psum | solution.py:108
  74.8 2.9 %convert_element_type.65 = f32[256,3,3,256]{3,0,2,1:T(8,128)} convert(bf16[256,3,3,256]{3,0,2,1:T(8,128)(2,1)} %all-reduce.14.cloned.1.call-done) | non-fusion elementwise | flops 589824 | bytes 3538944 | tf_op jit(solution)/shard_map/convert_element_type | solution.py:108
  79.3 0.5 copy.20
  80.6 0.5 copy.21
  81.2 0.9 pad_maximum_fusion
  82.4 1.8 %collective-permute-start.1 = (f32[1,1,512,256]{3,2,1,0:T(8,128)S(1)}, f32[1,1,512,256]{3,2,1,0:T(8,128)S(1)}, u32[]{:S(2)}, u32[]{:S(2)}) collective-permute-start(f32[1,1,512,256]{3,2,1,0:T(8,128)S(1)} %slice.157), channel_id=1, source_target_pairs={{0,1},{1,4},{4,5},{5,8},{8,9},{9,12},{12,13},{2,3},{3,6},{6,7},{7,... | collective-permute-start | bytes 1572872 | tf_op jit(solution)/shard_map/ppermute | solution.py:13
  84.1 0.6 dynamic-slice.8
  85.4 0.8 slice.155
  86.2 23.0 %all-reduce.10 = f32[256]{0:T(256)S(1)} all-reduce(bf16[256]{0:T(256)(128)(2,1)S(1)} %get-tuple-element.17), channel_id=4, replica_groups=mesh['groups'=2,'space'=4,'tm'=2,'col'=2] {'space','col'}, use_global_device_ids=true, to_apply=%region_6.7.clone | all-reduce | flops 256 | bytes 1536
  109.3 0.6 dynamic-slice_multiply_fusion
  109.9 1.3 %broadcast_multiply_fusion = f32[32,32]{1,0:T(8,128)} fusion(f32[32,32]{1,0:T(8,128)} %reduce-scatter.5.cloned.1.call-done), kind=kLoop, calls=%fused_computation.128 | loop fusion | flops 1024 | bytes 8192 | tf_op jit(solution)/shard_map/mul | solution.py:122
  111.2 0.8 fusion.23
  111.9 5.5 %reduce-scatter.3.cloned.1.call-done = f32[32,3,3,256]{3,0,2,1:T(8,128)} async-done(((f32[256,3,3,256]{3,0,2,1:T(8,128)}), f32[32,3,3,256]{3,0,2,1:T(8,128)}) %reduce-scatter.3.cloned.1.call-update) | async-done | bytes 294928 | tf_op jit(solution)/shard_map/reduce_scatter | solution.py:113
  117.5 1.7 %multiply_bitcast_fusion = f32[3,3,32,256]{3,2,1,0:T(8,128)} fusion(f32[32,3,3,256]{3,0,2,1:T(8,128)} %reduce-scatter.3.cloned.1.call-done), kind=kLoop, calls=%fused_computation.62 | loop fusion | flops 73728 | bytes 589824 | tf_op jit(solution)/shard_map/transpose | solution.py:121
  (76 shorter events, 7.2 us)
Async XLA Ops:
  8.0 2.4 %copy-start = (bf16[1,8,32,16]{2,3,1,0:T(8,128)(2,1)S(1)}, bf16[1,8,32,16]{2,3,1,0:T(8,128)(2,1)}, u32[]{:S(2)}) copy-start(bf16[1,8,32,16]{2,3,1,0:T(8,128)(2,1)} %param.12) | copy-start | bytes 24580
  8.0 15.2 %copy-start.2 = (bf16[1,2,512,256]{3,2,1,0:T(8,128)(2,1)S(1)}, bf16[1,2,512,256]{3,2,1,0:T(8,128)(2,1)}, u32[]{:S(2)}) copy-start(bf16[1,2,512,256]{3,2,1,0:T(8,128)(2,1)} %param.8) | copy-start | bytes 1572868
  8.0 66.8 %all-reduce.14.cloned.1.call-start = ((), (), s32[]{:S(2)}) async-start(), calls=%async_computation.3 | async-start | bytes 2359296 | tf_op jit(solution)/shard_map/psum | solution.py:108
  9.1 14.1 %collective-permute-start = (bf16[1,1,512,256]{3,2,1,0:T(8,128)(2,1)S(1)}, bf16[1,1,512,256]{3,2,1,0:T(8,128)(2,1)S(1)}, u32[]{:S(2)}, u32[]{:S(2)}) collective-permute-start(bf16[1,1,512,256]{3,2,1,0:T(8,128)(2,1)S(1)} %slice.129), channel_id=1, source_target_pairs={{1,0},{4,1},{5,4},{8,5},{9,8},{12,9},{13,12},{3,2},{6,3},{7,6},{10... | collective-permute-start | bytes 786440 | tf_op jit(solution)/shard_map/ppermute | solution.py:13
  23.2 3.8 %copy-start.1 = (bf16[3,3,256,256]{3,2,1,0:T(8,128)(2,1)S(1)}, bf16[3,3,256,256]{3,2,1,0:T(8,128)(2,1)}, u32[]{:S(2)}) copy-start(bf16[3,3,256,256]{3,2,1,0:T(8,128)(2,1)} %param.9) | copy-start | bytes 3538948
  23.3 3.8 %copy-start.12 = (f32[256]{0:T(256)S(1)}, f32[256]{0:T(256)}, u32[]{:S(2)}) copy-start(f32[256]{0:T(256)} %param.10) | copy-start | bytes 3076
  23.7 3.6 %copy-start.8 = (bf16[1,1,256,256]{3,2,1,0:T(8,128)(2,1)}, bf16[1,1,256,256]{3,2,1,0:T(8,128)(2,1)S(1)}, u32[]{:S(2)}) copy-start(bf16[1,1,256,256]{3,2,1,0:T(8,128)(2,1)S(1)} %slice.130) | copy-start | bytes 393220
  27.1 1.6 %copy-start.4 = (bf16[1,1,256,256]{3,2,1,0:T(8,128)(2,1)}, bf16[1,1,256,256]{3,2,1,0:T(8,128)(2,1)S(1)}, u32[]{:S(2)}) copy-start(bf16[1,1,256,256]{3,2,1,0:T(8,128)(2,1)S(1)} %slice.146) | copy-start | bytes 393220
  28.5 0.7 copy-start.10
  28.5 0.9 copy-start.11
  28.9 1.4 %copy-start.6 = (bf16[256,256]{1,0:T(8,128)(2,1)}, bf16[256,256]{1,0:T(8,128)(2,1)S(1)}, u32[]{:S(2)}) copy-start(bf16[256,256]{1,0:T(8,128)(2,1)S(1)} %get-tuple-element.20) | copy-start | bytes 393220
  28.9 1.0 copy-start.9
  30.4 1.4 %copy-start.5 = (bf16[1,1,256,256]{3,2,1,0:T(8,128)(2,1)S(1)}, bf16[1,1,256,256]{3,2,1,0:T(8,128)(2,1)}, u32[]{:S(2)}) copy-start(bf16[1,1,256,256]{3,2,1,0:T(8,128)(2,1)} %copy-done.4) | copy-start | bytes 393220
  31.3 1.8 %copy-start.7 = (bf16[256,256]{1,0:T(8,128)(2,1)S(1)}, bf16[256,256]{1,0:T(8,128)(2,1)}, u32[]{:S(2)}) copy-start(bf16[256,256]{1,0:T(8,128)(2,1)} %copy-done.6) | copy-start | bytes 393220
  32.0 1.0 copy-start.3
  33.1 76.8 %reduce-scatter.5.cloned.1.call-start = ((), (), s32[]{:S(2)}) async-start(), calls=%async_computation.5 | async-start | bytes 147456 | tf_op jit(solution)/shard_map/reduce_scatter | solution.py:114
  44.3 73.1 %reduce-scatter.3.cloned.1.call-start = ((), (), s32[]{:S(2)}) async-start(), calls=%async_computation.4 | async-start | bytes 2654208 | tf_op jit(solution)/shard_map/reduce_scatter | solution.py:113
  82.1 2.0 %copy-start.13 = (u32[32]{0:T(128)S(1)}, u32[32]{0:T(128)}, u32[]{:S(2)}) copy-start(u32[32]{0:T(128)} %constant.72) | copy-start | bytes 388
  82.4 28.8 %collective-permute-start.1 = (f32[1,1,512,256]{3,2,1,0:T(8,128)S(1)}, f32[1,1,512,256]{3,2,1,0:T(8,128)S(1)}, u32[]{:S(2)}, u32[]{:S(2)}) collective-permute-start(f32[1,1,512,256]{3,2,1,0:T(8,128)S(1)} %slice.157), channel_id=1, source_target_pairs={{0,1},{1,4},{4,5},{5,8},{8,9},{9,12},{12,13},{2,3},{3,6},{6,7},{7,... | collective-permute-start | bytes 1572872 | tf_op jit(solution)/shard_map/ppermute | solution.py:13
Sparse Core Ops, SparseCore 0:
  33.2 41.5 all-reduce.13
Sparse Core Ops, SparseCore 1:
  44.4 27.5 reduce-scatter.4
  77.8 39.6 reduce-scatter.2
where the time goes:
time: 127 us
  blocking collectives  45.8 us (36%)
  waiting for transfers between devices  36 us (28%)
  between operations  16.8 us (13%)
  local copies, waits for them, and re-layouts  9.32 us (7%)
  other arithmetic  9.3 us (7%)
  matrix products  6.28 us (5%)
  starting transfers between devices  3.18 us (3%)
    psum x1, waiting for transfers between devices, body(): lax.psum(kernel_term.astype(jnp.bfloat16), 'tm').astype(jnp.float32)  30.4 us
    unnamed x1, blocking collectives  23 us
    all_to_all x1, blocking collectives, body(): lax.all_to_all(latent_grad, ('space', 'col'), split_axis=1, concat_axis=2...  12.5 us
    psum x1, blocking collectives, body(): lax.psum(head_term.astype(jnp.bfloat16), 'tm').astype(jnp.float32)  10.3 us
    reduce_scatter x1, waiting for transfers between devices, body(): lax.psum_scatter(totals[0], ('space', 'col'), scatter_dimension=0, tiled=...  5.51 us
    slice x9, local copies, waits for them, and re-layouts, window_at(): padded[:, row_tap:row_tap + 2 * row_count:2, col_tap:col_tap + 2 * col_co...  3.7 us
    ppermute x2, starting transfers between devices, passed_along(): return lax.ppermute(x, axis, pairs)  3.06 us
    convert_element_type x1, other arithmetic, body(): lax.psum(kernel_term.astype(jnp.bfloat16), 'tm').astype(jnp.float32)  2.91 us
  transfers between devices with their start and end apart: 5, of which 2 were waited for; matrix products, arithmetic and copies ran while one was open for 10% of the time, Pallas kernels for 0%

commit v1 on v0

--- a/solution.py
+++ b/solution.py
@@ -105,7 +105,7 @@
     own_grad = own_grad.at[:, :1].add(rim_grad)
     x_grad = own_grad.astype(jnp.bfloat16)
     totals = (
-        lax.psum(kernel_term.astype(jnp.bfloat16), "tm").astype(jnp.float32),
+        jnp.sum(lax.all_gather(kernel_term.astype(jnp.bfloat16), "tm"), axis=0).astype(jnp.float32),
         lax.psum(head_term.astype(jnp.bfloat16), "tm").astype(jnp.float32),
         lax.psum(bias_term.astype(jnp.bfloat16), "tm").astype(jnp.float32),
     )

time: 127 us -> 121 us (0.953)
  waiting for transfers between devices: 36 us -> 30.1 us
  blocking collectives: 45.8 us -> 44.1 us
    psum x1 -> x0, waiting for transfers between devices: 30.4 us -> none  [body(): lax.psum(kernel_term.astype(jnp.bfloat16), 'tm').astype(jnp.float32)]
    all_gather x0 -> x1, waiting for transfers between devices: none -> 24.6 us  [body(): lax.all_gather(kernel_term.astype(jnp.bfloat16), 'tm')]
    reduce_sum x0 -> x1, other arithmetic: none -> 2.25 us  [body(): jnp.sum(lax.all_gather(kernel_term.astype(jnp.bfloat16), 'tm'), axis=0)]
  transfers between devices with their start and end apart: 5 -> 5, of which waited for: 2 -> 2; matrix products, arithmetic and copies ran while one was open for 10% -> 11% of each run, Pallas kernels for 0% -> 0%
where the time goes in v1:
time: 121 us; the launch traced here: 120 us
  blocking collectives  44.1 us (36%)
  waiting for transfers between devices  30.1 us (25%)
  between operations  16.8 us (14%)
  other arithmetic  10.3 us (9%)
  local copies, waits for them, and re-layouts  9.33 us (8%)
  matrix products  6.28 us (5%)
  starting transfers between devices  3.39 us (3%)
    all_gather x1, waiting for transfers between devices, body(): lax.all_gather(kernel_term.astype(jnp.bfloat16), 'tm')  24.6 us
    unnamed x1, blocking collectives  22.6 us
    all_to_all x1, blocking collectives, body(): lax.all_to_all(latent_grad, ('space', 'col'), split_axis=1, concat_axis=2...  12.5 us
    psum x1, blocking collectives, body(): lax.psum(head_term.astype(jnp.bfloat16), 'tm').astype(jnp.float32)  9.05 us
    reduce_scatter x1, waiting for transfers between devices, body(): lax.psum_scatter(totals[0], ('space', 'col'), scatter_dimension=0, tiled=...  5.51 us
    slice x9, local copies, waits for them, and re-layouts, window_at(): padded[:, row_tap:row_tap + 2 * row_count:2, col_tap:col_tap + 2 * col_co...  3.7 us
    ppermute x2, starting transfers between devices, passed_along(): return lax.ppermute(x, axis, pairs)  3.27 us
  transfers between devices with their start and end apart: 5, of which 2 were waited for; matrix products, arithmetic and copies ran while one was open for 11% of the time, Pallas kernels for 0%

profile of v1, /device:TPU:0, one launch (start us, length us, event | category | flops | bytes accessed | tf_op | source)
XLA Modules:
  0.0 120.2 jit_solution(10892575549093298322)
XLA Ops:
  8.1 1.0 slice.129
  9.1 1.3 %collective-permute-start = (bf16[1,1,512,256]{3,2,1,0:T(8,128)(2,1)S(1)}, bf16[1,1,512,256]{3,2,1,0:T(8,128)(2,1)S(1)}, u32[]{:S(2)}, u32[]{:S(2)}) collective-permute-start(bf16[1,1,512,256]{3,2,1,0:T(8,128)(2,1)S(1)} %slice.129), channel_id=1, source_target_pairs={{1,0},{4,1},{5,4},{8,5},{9,8},{12,9},{13,12},{3,2},{6,3},{7,6},{10... | collective-permute-start | bytes 786440 | tf_op jit(solution)/shard_map/ppermute | solution.py:13
  10.5 12.5 %all_to_all.4 = bf16[8,2,256]{2,1,0:T(2,128)(2,1)S(1)} all-to-all(bf16[8,2,256]{2,1,0:T(2,128)(2,1)S(1)} %reshape.200), channel_id=1, replica_groups=mesh['groups'=2,'space'=4,'tm'=2,'col'=2] {'space','col'}, dimensions={0} | all-to-all | bytes 16384 | tf_op jit(solution)/shard_map/all_to_all | solution.py:61
  23.3 0.4 slice.130
  23.7 0.4 slice.132
  24.1 0.4 slice.134
  24.5 0.4 slice.136
  24.9 0.4 slice.138
  25.3 0.4 slice.140
  25.8 0.4 slice.142
  26.2 0.4 slice.144
  26.6 0.4 slice.146
  29.4 0.2 fusion.85
  29.6 0.3 copy-done.9
  32.0 1.0 copy-done.3
  33.4 9.1 %all-reduce.11 = (bf16[256,32]{1,0:T(8,128)(2,1)S(1)}, bf16[256]{0:T(256)(128)(2,1)S(1)}) all-reduce(bf16[256,32]{1,0:T(8,128)(2,1)S(1)} %convolution_convert_fusion.9, bf16[256]{0:T(256)(128)(2,1)S(1)} %get-tuple-element.22), channel_id=1, replica_groups=mesh['groups'=2,'space'=4,'tm'=2,'col'=2] {'tm'}, use_global_device_ids=true, to_apply=%region_2.3 | all-reduce | flops 8448 | bytes 33792 | tf_op jit(solution)/shard_map/psum | solution.py:109
  42.4 0.7 convert_element_type.76
  43.2 24.6 %all-gather.2.cloned.1.call-done = bf16[2,256,3,3,256]{4,1,3,2,0:T(8,128)(2,1)} async-done(((bf16[1,256,3,3,256]{4,1,3,2,0:T(8,128)(2,1)}), bf16[2,256,3,3,256]{4,1,3,2,0:T(8,128)(2,1)}) %all-gather.2.cloned.1.call-update) | async-done | bytes 2359312 | tf_op jit(solution)/shard_map/all_gather | solution.py:108
  67.7 2.3 %reduce_sum.24 = bf16[256,3,3,256]{3,0,2,1:T(8,128)(2,1)S(1)} reduce(bf16[2,256,3,3,256]{4,1,3,2,0:T(8,128)(2,1)} %all-gather.2.cloned.1.call-done, bf16[]{:T(256)} %constant.41.clone.1), dimensions={0}, to_apply=%region_0.1 | reduce | flops 589824 | bytes 3538946 | tf_op jit(solution)/shard_map/reduce_sum | solution.py:108
  70.0 1.6 %convert_element_type.74 = f32[256,3,3,256]{3,0,2,1:T(8,128)} convert(bf16[256,3,3,256]{3,0,2,1:T(8,128)(2,1)S(1)} %reduce_sum.24) | non-fusion elementwise | flops 589824 | bytes 3538944 | tf_op jit(solution)/shard_map/convert_element_type | solution.py:108
  73.2 0.5 copy.20
  74.6 0.5 copy.21
  75.1 0.9 pad_maximum_fusion
  76.3 2.0 %collective-permute-start.1 = (f32[1,1,512,256]{3,2,1,0:T(8,128)S(1)}, f32[1,1,512,256]{3,2,1,0:T(8,128)S(1)}, u32[]{:S(2)}, u32[]{:S(2)}) collective-permute-start(f32[1,1,512,256]{3,2,1,0:T(8,128)S(1)} %slice.157), channel_id=1, source_target_pairs={{0,1},{1,4},{4,5},{5,8},{8,9},{9,12},{12,13},{2,3},{3,6},{6,7},{7,... | collective-permute-start | bytes 1572872 | tf_op jit(solution)/shard_map/ppermute | solution.py:13
  78.3 0.6 dynamic-slice.8
  79.5 0.8 slice.155
  80.4 22.6 %all-reduce.10 = f32[256]{0:T(256)S(1)} all-reduce(bf16[256]{0:T(256)(128)(2,1)S(1)} %get-tuple-element.17), channel_id=4, replica_groups=mesh['groups'=2,'space'=4,'tm'=2,'col'=2] {'space','col'}, use_global_device_ids=true, to_apply=%region_6.7.clone | all-reduce | flops 256 | bytes 1536
  102.9 0.6 dynamic-slice_multiply_fusion
  103.5 1.3 %broadcast_multiply_fusion = f32[32,32]{1,0:T(8,128)} fusion(f32[32,32]{1,0:T(8,128)} %reduce-scatter.5.cloned.1.call-done), kind=kLoop, calls=%fused_computation.128 | loop fusion | flops 1024 | bytes 8192 | tf_op jit(solution)/shard_map/mul | solution.py:122
  104.8 0.8 fusion.23
  105.6 5.5 %reduce-scatter.3.cloned.1.call-done = f32[32,3,3,256]{3,0,2,1:T(8,128)} async-done(((f32[256,3,3,256]{3,0,2,1:T(8,128)}), f32[32,3,3,256]{3,0,2,1:T(8,128)}) %reduce-scatter.3.cloned.1.call-update) | async-done | bytes 294928 | tf_op jit(solution)/shard_map/reduce_scatter | solution.py:113
  111.1 1.7 %multiply_bitcast_fusion = f32[3,3,32,256]{3,2,1,0:T(8,128)} fusion(f32[32,3,3,256]{3,0,2,1:T(8,128)} %reduce-scatter.3.cloned.1.call-done), kind=kLoop, calls=%fused_computation.62 | loop fusion | flops 73728 | bytes 589824 | tf_op jit(solution)/shard_map/transpose | solution.py:121
  (77 shorter events, 7.5 us)
Async XLA Ops:
  8.0 2.4 %copy-start = (bf16[1,8,32,16]{2,3,1,0:T(8,128)(2,1)S(1)}, bf16[1,8,32,16]{2,3,1,0:T(8,128)(2,1)}, u32[]{:S(2)}) copy-start(bf16[1,8,32,16]{2,3,1,0:T(8,128)(2,1)} %param.12) | copy-start | bytes 24580
  8.0 15.2 %copy-start.2 = (bf16[1,2,512,256]{3,2,1,0:T(8,128)(2,1)S(1)}, bf16[1,2,512,256]{3,2,1,0:T(8,128)(2,1)}, u32[]{:S(2)}) copy-start(bf16[1,2,512,256]{3,2,1,0:T(8,128)(2,1)} %param.8) | copy-start | bytes 1572868
  8.0 59.7 %all-gather.2.cloned.1.call-start = ((), (), s32[]{:S(2)}) async-start(), calls=%async_computation.3 | async-start | bytes 3538944 | tf_op jit(solution)/shard_map/all_gather | solution.py:108
  9.1 14.1 %collective-permute-start = (bf16[1,1,512,256]{3,2,1,0:T(8,128)(2,1)S(1)}, bf16[1,1,512,256]{3,2,1,0:T(8,128)(2,1)S(1)}, u32[]{:S(2)}, u32[]{:S(2)}) collective-permute-start(bf16[1,1,512,256]{3,2,1,0:T(8,128)(2,1)S(1)} %slice.129), channel_id=1, source_target_pairs={{1,0},{4,1},{5,4},{8,5},{9,8},{12,9},{13,12},{3,2},{6,3},{7,6},{10... | collective-permute-start | bytes 786440 | tf_op jit(solution)/shard_map/ppermute | solution.py:13
  23.2 3.8 %copy-start.1 = (bf16[3,3,256,256]{3,2,1,0:T(8,128)(2,1)S(1)}, bf16[3,3,256,256]{3,2,1,0:T(8,128)(2,1)}, u32[]{:S(2)}) copy-start(bf16[3,3,256,256]{3,2,1,0:T(8,128)(2,1)} %param.9) | copy-start | bytes 3538948
  23.3 3.8 %copy-start.12 = (f32[256]{0:T(256)S(1)}, f32[256]{0:T(256)}, u32[]{:S(2)}) copy-start(f32[256]{0:T(256)} %param.10) | copy-start | bytes 3076
  23.7 3.6 %copy-start.8 = (bf16[1,1,256,256]{3,2,1,0:T(8,128)(2,1)}, bf16[1,1,256,256]{3,2,1,0:T(8,128)(2,1)S(1)}, u32[]{:S(2)}) copy-start(bf16[1,1,256,256]{3,2,1,0:T(8,128)(2,1)S(1)} %slice.130) | copy-start | bytes 393220
  27.1 1.6 %copy-start.4 = (bf16[1,1,256,256]{3,2,1,0:T(8,128)(2,1)}, bf16[1,1,256,256]{3,2,1,0:T(8,128)(2,1)S(1)}, u32[]{:S(2)}) copy-start(bf16[1,1,256,256]{3,2,1,0:T(8,128)(2,1)S(1)} %slice.146) | copy-start | bytes 393220
  28.5 0.7 copy-start.10
  28.5 0.9 copy-start.11
  28.9 1.4 %copy-start.6 = (bf16[256,256]{1,0:T(8,128)(2,1)}, bf16[256,256]{1,0:T(8,128)(2,1)S(1)}, u32[]{:S(2)}) copy-start(bf16[256,256]{1,0:T(8,128)(2,1)S(1)} %get-tuple-element.20) | copy-start | bytes 393220
  28.9 1.0 copy-start.9
  30.4 1.4 %copy-start.5 = (bf16[1,1,256,256]{3,2,1,0:T(8,128)(2,1)S(1)}, bf16[1,1,256,256]{3,2,1,0:T(8,128)(2,1)}, u32[]{:S(2)}) copy-start(bf16[1,1,256,256]{3,2,1,0:T(8,128)(2,1)} %copy-done.4) | copy-start | bytes 393220
  31.3 1.8 %copy-start.7 = (bf16[256,256]{1,0:T(8,128)(2,1)S(1)}, bf16[256,256]{1,0:T(8,128)(2,1)}, u32[]{:S(2)}) copy-start(bf16[256,256]{1,0:T(8,128)(2,1)} %copy-done.6) | copy-start | bytes 393220
  32.0 1.0 copy-start.3
  33.1 70.4 %reduce-scatter.5.cloned.1.call-start = ((), (), s32[]{:S(2)}) async-start(), calls=%async_computation.5 | async-start | bytes 147456 | tf_op jit(solution)/shard_map/reduce_scatter | solution.py:114
  43.1 68.0 %reduce-scatter.3.cloned.1.call-start = ((), (), s32[]{:S(2)}) async-start(), calls=%async_computation.4 | async-start | bytes 2654208 | tf_op jit(solution)/shard_map/reduce_scatter | solution.py:113
  76.0 2.2 %copy-start.13 = (u32[32]{0:T(128)S(1)}, u32[32]{0:T(128)}, u32[]{:S(2)}) copy-start(u32[32]{0:T(128)} %constant.73) | copy-start | bytes 388
  76.3 28.6 %collective-permute-start.1 = (f32[1,1,512,256]{3,2,1,0:T(8,128)S(1)}, f32[1,1,512,256]{3,2,1,0:T(8,128)S(1)}, u32[]{:S(2)}, u32[]{:S(2)}) collective-permute-start(f32[1,1,512,256]{3,2,1,0:T(8,128)S(1)} %slice.157), channel_id=1, source_target_pairs={{0,1},{1,4},{4,5},{5,8},{8,9},{9,12},{12,13},{2,3},{3,6},{6,7},{7,... | collective-permute-start | bytes 1572872 | tf_op jit(solution)/shard_map/ppermute | solution.py:13
Sparse Core Ops, SparseCore 0:
  33.2 34.4 all-gather.1
Sparse Core Ops, SparseCore 1:
  43.2 27.5 reduce-scatter.4
  73.1 38.0 reduce-scatter.2
